TPU v7x, 32 devices: a whole 2x2x4 slice. The times are simulated.
32 devices in a mesh: ctx: 16 (over z, x, core), fsdp: 2 (over y).
Axes of the slice: x: 2, y: 2, z: 4, core: 2. Of those that a mesh axis runs over, the one named last changes fastest.
Arguments:
- tokens: bfloat16 [2, 4096, 1024], P('fsdp', 'ctx'), may hold values from -6 to 6
- cotangent: bfloat16 [2, 4096, 1024], P('fsdp', 'ctx'), may hold values from -6 to 6
- w_qkv: bfloat16 [1024, 3072], P('fsdp'), may hold values from -0.25 to 0.25
- w_up: bfloat16 [1024, 4096], P('fsdp'), may hold values from -0.1875 to 0.1875
- w_out: bfloat16 [1024, 1024], P('fsdp'), may hold values from -0.375 to 0.375
- w_down: bfloat16 [4096, 1024], P('fsdp'), may hold values from -0.09375 to 0.09375
- b_qkv: bfloat16 [3072], replicated, may hold values from -0.59765625 to 0.59765625
- b_up: bfloat16 [4096], replicated, may hold values from -3 to 3
- b_out: bfloat16 [1024], replicated, may hold values from -2 to 2
- b_down: bfloat16 [1024], replicated, may hold values from -2 to 2
- ln_gain: bfloat16 [1024], replicated, may hold values from 0.5 to 1.5
- ln_bias: bfloat16 [1024], replicated, may hold values from -2 to 2
- block_table: int32 [2, 32], P('fsdp'), may hold values from 0 to 31, each once within a row
- seg_ids: int32 [2, 4096], P('fsdp'), may hold values from 0 to 2, as said below
- positions: int32 [2, 4096], P('fsdp'), may hold values from 0 to 4094, as said below
Outputs:
- output: bfloat16 [2, 4096, 1024], P('fsdp', 'ctx')
- input_grad: bfloat16 [2, 4096, 1024], P('fsdp', 'ctx')
- w_qkv_grad: float32 [1024, 3072], P('fsdp')
- w_up_grad: float32 [1024, 4096], P('fsdp')
- w_out_grad: float32 [1024, 1024], P('fsdp')
- w_down_grad: float32 [4096, 1024], P('fsdp')
- b_qkv_grad: float32 [3072], replicated
- b_up_grad: float32 [4096], replicated
- b_out_grad: float32 [1024], replicated
- b_down_grad: float32 [1024], replicated
- ln_gain_grad: float32 [1024], replicated
- ln_bias_grad: float32 [1024], replicated
Inputs may be any that keep to these rules, and one draw needn't show every extreme that they name: Storage block b of group g (rows b * 128 to b * 128 + 127 along the token dimension) holds the group's logical block block_table[g, b]; each row is a permutation. `seg_ids`: in logical order, segment 0 (the prompt) is one run of 2048 tokens and each segment 1 to 2 (a continuation) one run of 1024 tokens; the runs stand in any order. `positions`: the prompt counts from 0; each continuation counts from 2048 plus an offset of its own below 1024.
All inputs are finite; a program needn't handle non-finite values.
Results may differ from a plain program's by a relative error of at most 0.015.
The roundings to bfloat16 on the way count: a program that leaves them out, or rounds other values in their place, can miss the bound.
Values may be sent and summed in bfloat16 or wider, within the bound.
A program may use at most 448 MiB of HBM per device.

v0:
```python
import jax
import jax.numpy as jnp
from jax import lax
from jax.sharding import PartitionSpec as P

D = 1024
HEADS = 16
HDIM = 64
FF = 4096
ROT = 16


eps_norm = 1e-05


def layer_norm(inputs, norm_gain, norm_shift):
    centered = inputs - jnp.mean(inputs, axis=-1, keepdims=True)
    variance = jnp.mean(centered * centered, axis=-1, keepdims=True)
    return centered * lax.rsqrt(variance + eps_norm) * norm_gain + norm_shift


def angles_of(placed):
    frequency = 10000.0 ** (-jnp.arange(0, ROT, 2, dtype=jnp.float32) / ROT)
    phases = placed.astype(jnp.float32)[:, None, None] * frequency[None, None, :]
    return (jnp.cos(phases), jnp.sin(phases))


def rotate(values, cos_terms, sin_terms):
    halfway = ROT // 2
    first_half = values[..., :halfway]
    second_half = values[..., halfway:ROT]
    return jnp.concatenate(
        [
            first_half * cos_terms - second_half * sin_terms,
            second_half * cos_terms + first_half * sin_terms,
            values[..., ROT:],
        ],
        axis=-1,
    )


def allowed_pairs(query_seg, query_order, key_seg, key_order):
    same_run = (query_seg[:, None] == key_seg[None, :]) & (
        key_order[None, :] <= query_order[:, None]
    )
    from_prompt = (key_seg[None, :] == 0) & (query_seg[:, None] != 0)
    return same_run | from_prompt


def exact_gelu(values):
    return jax.nn.gelu(values, approximate=False)


def contract_last(left_side, right_side):
    return lax.dot_general(
        left_side, right_side, (((1,), (1,)), ((), ())), preferred_element_type=jnp.float32
    )


def contract_first(left_side, right_side):
    return lax.dot_general(
        left_side, right_side, (((0,), (0,)), ((), ())), preferred_element_type=jnp.float32
    )


def local(
    tokens,
    cotangent,
    w_qkv,
    w_up,
    w_out,
    w_down,
    b_qkv,
    b_up,
    b_out,
    b_down,
    ln_gain,
    ln_bias,
    block_table,
    seg_ids,
    positions,
):
    shard_count = lax.axis_size("fsdp")
    ctx_count = lax.axis_size("ctx")
    inputs = tokens[0].astype(jnp.float32)
    tok_rows = inputs.shape[0]
    table_row = block_table[0]
    block_rows = tok_rows * ctx_count // table_row.shape[0]
    all_order = (
        table_row[:, None] * block_rows + jnp.arange(block_rows, dtype=jnp.int32)[None, :]
    ).reshape(-1)
    all_seg = seg_ids[0].reshape(-1, block_rows)[table_row].reshape(-1)
    all_place = positions[0].reshape(-1, block_rows)[table_row].reshape(-1)
    own_first = lax.axis_index("ctx") * tok_rows
    own_order = lax.dynamic_slice_in_dim(all_order, own_first, tok_rows)
    own_seg = lax.dynamic_slice_in_dim(all_seg, own_first, tok_rows)
    own_place = lax.dynamic_slice_in_dim(all_place, own_first, tok_rows)
    cos_own, sin_own = angles_of(own_place)
    score_scale = HDIM ** (-0.5)
    heads_shape = (tok_rows, HEADS, HDIM)
    norm_out, norm_pull = jax.vjp(
        layer_norm, inputs, ln_gain.astype(jnp.float32), ln_bias.astype(jnp.float32)
    )
    normed = norm_out.astype(jnp.bfloat16)
    pieces = (
        lax.all_gather(w_qkv, "fsdp", axis=0, tiled=True),
        lax.all_gather(w_up, "fsdp", axis=0, tiled=True),
    )
    piece_rows = pieces[0].shape[0]
    columns = normed
    merged_part = jnp.dot(columns, pieces[0], preferred_element_type=jnp.float32)
    up_part = jnp.dot(columns, pieces[1], preferred_element_type=jnp.float32)
    merged_all = merged_part + b_qkv.astype(jnp.float32)
    up_proj = up_part + b_up.astype(jnp.float32)

    def turn_own(values):
        return rotate(values, cos_own, sin_own)

    query_turned, turn_pull = jax.vjp(turn_own, merged_all[:, :D].reshape(heads_shape))
    queries = query_turned.astype(jnp.bfloat16)
    keys_own = turn_own(merged_all[:, D : 2 * D].reshape(heads_shape)).astype(jnp.bfloat16)
    values_own = merged_all[:, 2 * D :].reshape(heads_shape).astype(jnp.bfloat16)

    def split_heads(pieces):
        piece_rows = pieces[0].shape[0]
        return (
            pieces[0].reshape(piece_rows, HEADS, HDIM),
            pieces[1].reshape(piece_rows, HEADS, HDIM),
        )

    def mask_keys():
        return allowed_pairs(own_seg, own_order, all_seg, all_order)

    attn_start = (jnp.zeros(heads_shape, jnp.float32), jnp.zeros((HEADS, tok_rows), jnp.float32))
    keys_flat = keys_own.reshape(tok_rows, D)
    values_flat = values_own.reshape(tok_rows, D)
    pieces = (
        lax.all_gather(keys_flat, "ctx", axis=0, tiled=True),
        lax.all_gather(values_flat, "ctx", axis=0, tiled=True),
    )
    make_kv = lambda: split_heads(pieces)
    allowed = mask_keys()

    def forward_compute(running):
        keys_piece, values_piece = make_kv()
        scores = (
            jnp.einsum("qhd,khd->hqk", queries, keys_piece, preferred_element_type=jnp.float32)
            * score_scale
        )
        weights = jnp.where(allowed[None], jnp.exp(scores), 0.0)
        mixed = jnp.einsum(
            "hqk,khd->qhd",
            weights.astype(jnp.bfloat16),
            values_piece,
            preferred_element_type=jnp.float32,
        )
        return (mixed, jnp.sum(weights, axis=-1))

    unnormed, totals = lax.cond(
        jnp.any(allowed), forward_compute, lambda running: running, attn_start
    )
    totals_rows = jnp.transpose(totals)[:, :, None]
    attn_float = unnormed / totals_rows
    attended = attn_float.astype(jnp.bfloat16).reshape(tok_rows, D)
    gelu_value, gelu_pull = jax.vjp(exact_gelu, up_proj)
    gated = gelu_value.astype(jnp.bfloat16)
    slice_in = D // shard_count
    slice_ff = FF // shard_count
    joined = jnp.concatenate(
        [
            attended.reshape(tok_rows, shard_count, slice_in),
            gated.reshape(tok_rows, shard_count, slice_ff),
        ],
        axis=2,
    ).reshape(tok_rows, D + FF)
    local_out = jnp.concatenate([w_out, w_down], axis=0)
    columns = joined
    branch_sum = jnp.dot(
        columns,
        lax.all_gather(local_out, "fsdp", axis=0, tiled=True),
        preferred_element_type=jnp.float32,
    )
    output = (inputs + branch_sum + b_out.astype(jnp.float32) + b_down.astype(jnp.float32)).astype(
        jnp.bfloat16
    )
    grad_out = cotangent[0]
    grad_float = grad_out.astype(jnp.float32)
    grad_joined = contract_last(grad_out, lax.all_gather(local_out, "fsdp", axis=0, tiled=True))
    grad_split = grad_joined.reshape(tok_rows, shard_count, slice_in + slice_ff)
    grad_attn = grad_split[:, :, :slice_in].reshape(heads_shape)
    grad_gated = grad_split[:, :, slice_in:].reshape(tok_rows, FF)
    grad_up = gelu_pull(grad_gated)[0].astype(jnp.bfloat16)
    grad_scaled = (grad_attn / totals_rows).astype(jnp.bfloat16)
    row_delta = jnp.sum(grad_attn * attn_float, axis=-1) / jnp.transpose(totals)
    delta_heads = jnp.transpose(row_delta)
    query_pieces = (
        lax.all_gather(keys_flat, "ctx", axis=0, tiled=True),
        lax.all_gather(values_flat, "ctx", axis=0, tiled=True),
    )
    query_make_kv = lambda: split_heads(query_pieces)
    query_allowed = mask_keys()

    def query_compute(running):
        keys_piece, values_piece = query_make_kv()
        scores = (
            jnp.einsum("qhd,khd->hqk", queries, keys_piece, preferred_element_type=jnp.float32)
            * score_scale
        )
        weights = jnp.where(query_allowed[None], jnp.exp(scores), 0.0)
        products = jnp.einsum(
            "qhd,khd->hqk", grad_scaled, values_piece, preferred_element_type=jnp.float32
        )
        slopes = (weights * (products - delta_heads[:, :, None])).astype(jnp.bfloat16)
        return (
            jnp.einsum("hqk,khd->qhd", slopes, keys_piece, preferred_element_type=jnp.float32)
            * score_scale
        )

    grad_query = lax.cond(
        jnp.any(query_allowed),
        query_compute,
        lambda running: running,
        jnp.zeros(heads_shape, jnp.float32),
    )
    all_delta = lax.all_gather(delta_heads, "ctx", axis=1, tiled=True)
    queries_flat = queries.reshape(tok_rows, D)
    scaled_flat = grad_scaled.reshape(tok_rows, D)
    key_pieces = (
        lax.all_gather(queries_flat, "ctx", axis=0, tiled=True),
        lax.all_gather(scaled_flat, "ctx", axis=0, tiled=True),
    )
    piece_rows = key_pieces[0].shape[0]
    query_piece = key_pieces[0].reshape(piece_rows, HEADS, HDIM)
    grad_piece = key_pieces[1].reshape(piece_rows, HEADS, HDIM)
    key_allowed = allowed_pairs(all_seg, all_order, own_seg, own_order)

    def key_compute(running):
        scores = (
            jnp.einsum("qhd,khd->hqk", query_piece, keys_own, preferred_element_type=jnp.float32)
            * score_scale
        )
        weights = jnp.where(key_allowed[None], jnp.exp(scores), 0.0)
        products = jnp.einsum(
            "qhd,khd->hqk", grad_piece, values_own, preferred_element_type=jnp.float32
        )
        slopes = (weights * (products - all_delta[:, :, None])).astype(jnp.bfloat16)
        grad_keys = (
            jnp.einsum("hqk,qhd->khd", slopes, query_piece, preferred_element_type=jnp.float32)
            * score_scale
        )
        grad_values = jnp.einsum(
            "hqk,qhd->khd",
            weights.astype(jnp.bfloat16),
            grad_piece,
            preferred_element_type=jnp.float32,
        )
        return (grad_keys, grad_values)

    grad_keys, grad_values = lax.cond(
        jnp.any(key_allowed),
        key_compute,
        lambda running: running,
        (jnp.zeros(heads_shape, jnp.float32), jnp.zeros(heads_shape, jnp.float32)),
    )
    grad_merged = jnp.concatenate(
        [
            turn_pull(grad_query)[0].reshape(tok_rows, D),
            turn_pull(grad_keys)[0].reshape(tok_rows, D),
            grad_values.reshape(tok_rows, D),
        ],
        axis=1,
    ).astype(jnp.bfloat16)
    columns = contract_last(
        grad_merged, lax.all_gather(w_qkv, "fsdp", axis=0, tiled=True)
    ) + contract_last(grad_up, lax.all_gather(w_up, "fsdp", axis=0, tiled=True))
    grad_normed = columns
    grad_inputs, grad_gain, grad_shift = norm_pull(grad_normed)
    input_grad = (grad_float + grad_inputs).astype(jnp.bfloat16)
    columns = normed
    in_share = lax.psum_scatter(
        jnp.concatenate(
            [contract_first(columns, grad_merged), contract_first(columns, grad_up)], axis=1
        ).astype(jnp.bfloat16),
        "fsdp",
        scatter_dimension=0,
        tiled=True,
    )
    columns = joined
    out_share = lax.psum_scatter(
        contract_first(columns, grad_out).astype(jnp.bfloat16),
        "fsdp",
        scatter_dimension=0,
        tiled=True,
    )
    in_total, out_total = (
        lax.psum(in_share, "ctx").astype(jnp.float32),
        lax.psum(out_share, "ctx").astype(jnp.float32),
    )
    small_sums = lax.psum(
        (
            jnp.sum(grad_merged, axis=0, dtype=jnp.float32),
            jnp.sum(grad_up, axis=0, dtype=jnp.float32),
            jnp.sum(grad_float, axis=0),
            grad_gain,
            grad_shift,
        ),
        ("ctx", "fsdp"),
    )
    return (
        output[None],
        input_grad[None],
        in_total[:, : 3 * D],
        in_total[:, 3 * D :],
        out_total[:slice_in],
        out_total[slice_in:],
        small_sums[0],
        small_sums[1],
        small_sums[2],
        small_sums[2],
        small_sums[3],
        small_sums[4],
    )


def solution(mesh):
    in_specs = (
        P("fsdp", "ctx", None),
        P("fsdp", "ctx", None),
        P("fsdp", None),
        P("fsdp", None),
        P("fsdp", None),
        P("fsdp", None),
        P(),
        P(),
        P(),
        P(),
        P(),
        P(),
        P("fsdp", None),
        P("fsdp", None),
        P("fsdp", None),
    )
    out_specs = (
        P("fsdp", "ctx", None),
        P("fsdp", "ctx", None),
        P("fsdp", None),
        P("fsdp", None),
        P("fsdp", None),
        P("fsdp", None),
        P(),
        P(),
        P(),
        P(),
        P(),
        P(),
    )
    return jax.shard_map(local, mesh=mesh, in_specs=in_specs, out_specs=out_specs, check_vma=False)
```

profile of v0, /device:TPU:25, one launch (start us, length us, event | category | flops | bytes accessed | tf_op | source)
XLA Modules:
  0.0 1197.5 jit_solution(17895208468700812791)
XLA Ops:
  7.2 0.7 all-gather.8.cloned.1.call-update
  8.0 5.4 pad_maximum_fusion.1
  15.5 75.5 %all-gather.8.cloned.1.call-done = bf16[1024,3072]{1,0:T(8,128)(2,1)} async-done(((bf16[512,3072]{1,0:T(8,128)(2,1)}), bf16[1024,3072]{1,0:T(8,128)(2,1)}) %all-gather.8.cloned.1.call-update) | async-done | bytes 6291472 | tf_op jit(solution)/shard_map/all_gather | solution.py:106
  91.0 4.7 convolution_add_fusion.1
  95.7 1.7 copy-done.12
  97.5 1.3 copy.42
  99.1 1.3 slice.67
  100.5 1.1 multiply_subtract_fusion
  101.6 0.8 maximum_convert_fusion
  102.5 2.4 slice.93
  105.6 0.8 maximum_convert_fusion.1
  107.4 3.1 fusion.69
  111.2 111.4 %all-gather.16.cloned.1.call-done = bf16[5120,1024]{1,0:T(8,128)(2,1)} async-done(((bf16[2560,1024]{1,0:T(8,128)(2,1)}), bf16[5120,1024]{1,0:T(8,128)(2,1)}) %all-gather.16.cloned.1.call-update) | async-done | bytes 10485776 | tf_op jit(solution)/shard_map/all_gather | solution.py:180
  222.6 5.9 fusion.56
  228.6 2.3 copy-done.10
  231.0 71.0 %all-gather.10.cloned.1.call-done = bf16[4096,1024]{0,1:T(8,128)(2,1)} async-done(((bf16[256,1024]{0,1:T(8,128)(2,1)}), bf16[4096,1024]{0,1:T(8,128)(2,1)}) %all-gather.10.cloned.1.call-update) | async-done | bytes 8388624 | tf_op jit(solution)/shard_map/all_gather | solution.py:138
  302.0 75.2 %all-gather.12.cloned.1.call-done = bf16[4096,1024]{1,0:T(8,128)(2,1)} async-done(((bf16[256,1024]{1,0:T(8,128)(2,1)}), bf16[4096,1024]{1,0:T(8,128)(2,1)}) %all-gather.12.cloned.1.call-update) | async-done | bytes 8388624 | tf_op jit(solution)/shard_map/all_gather | solution.py:139
  377.3 70.7 %conditional.3 = (f32[256,16,64]{0,2,1:T(8,128)S(1)}, f32[16,256]{1,0:T(8,128)S(1)}) conditional(s32[]{:T(128)} %convert_element_type.116, () %tuple.32, (pred[256,4096]{1,0:T(8,128)(4,1)}, bf16[4096,1024]{0,1:T(8,128)(2,1)}, bf16[256,16,64]{0,2,1:T(8,128)(2,1)S(1)}, bf16[4096,1024]{1,0:T(8,128)(2,1)}) %tuple.101), branch_computations={%region_3.0_spmd, %region_4.6_spmd} | conditional | flops 4395626496 | bytes 171458576 | solution.py:159
  377.4 32.6 %fusion = (f32[16,256]{1,0:T(8,128)S(1)}, f32[16,256,4096]{2,1,0:T(8,128)}) fusion(pred[256,4096]{1,0:T(8,128)(4,1)} %get-tuple-element.40, bf16[256,16,64]{0,2,1:T(8,128)(2,1)S(1)} %get-tuple-element.41, bf16[4096,16,64]{0,2,1:T(8,128)(2,1)} %bitcast.148), kind=kOutput, calls=%fused_computation.3 | convolution fusion | flops 2197811200 | bytes 77086720 | tf_op jit(solution)/shard_map/cond/branch_1_fun/qhd,khd->hqk/dot_general | solution.py:147
  410.1 11.9 copy.44
  422.0 26.0 %fusion.5 = f32[256,16,64]{0,2,1:T(8,128)S(1)} fusion(bf16[4096,16,64]{0,2,1:T(8,128)(2,1)} %bitcast.155, f32[16,256,4096]{2,1,0:T(8,128)} %get-tuple-element.118, pred[256,4096]{1,0:T(8,128)(4,1)} %get-tuple-element.40), kind=kOutput, calls=%fused_computation.7 | convolution fusion | flops 2197815296 | bytes 77594624 | tf_op jit(solution)/shard_map/cond/branch_1_fun/hqk,khd->qhd/dot_general | solution.py:151
  448.0 0.9 fusion.53
  449.2 4.5 slice.74
  453.6 5.6 copy.53
  459.2 23.1 %all-gather.14.cloned.1.call-done = bf16[1024,4096]{1,0:T(8,128)(2,1)} async-done(((bf16[512,4096]{1,0:T(8,128)(2,1)}), bf16[1024,4096]{1,0:T(8,128)(2,1)}) %all-gather.14.cloned.1.call-update) | async-done | bytes 8388624 | tf_op jit(solution)/shard_map/all_gather | solution.py:107
  482.3 16.0 %convert_reduce_fusion = (f32[4096]{0:T(1024)}, bf16[256,4096]{1,0:T(8,128)(2,1)}, f32[256,4096]{1,0:T(8,128)S(1)}, f32[256,4096]{1,0:T(8,128)S(1)}) fusion(f32[256,4096]{1,0:T(8,128)} %copy.53, f32[4096]{0:T(1024)S(1)} %convert_element_type.127, bf16[1024,4096]{1,0:T(8,128)(2,1)} %all-gather.14.cloned.1.call-done, bf16[1,256,1024]{2,1,0:T(8,128)(2,1)S(1)} %copy-done.4, ...), kind=kOutput, calls=%fused_computation.37 | convolution fusion | flops 2227695616 | bytes 23635968 | tf_op jit(solution)/shard_map/dot_general | solution.py:112
  498.3 2.0 multiply_convert_fusion.2
  500.4 4.5 reshape.300
  504.8 1.2 divide_convert_fusion
  506.1 1.3 copy.45
  507.4 4.0 pad_maximum_fusion.2
  511.8 1.5 copy-done.6
  513.3 5.5 convolution_convert_fusion
  519.3 5.3 fusion.68
  525.2 7.6 convolution_convert_fusion.1
  532.8 75.8 %conditional.4 = (f32[256,16,64]{0,2,1:T(8,128)S(1)}) conditional(s32[]{:T(128)} %convert_element_type.116, () %tuple.34, (pred[256,4096]{1,0:T(8,128)(4,1)}, bf16[4096,1024]{0,1:T(8,128)(2,1)}, bf16[256,16,64]{0,2,1:T(8,128)(2,1)S(1)}, bf16[4096,1024]{1,0:T(8,128)(2,1)}, bf16[256,16,64]{0,2,1:T(8,128)(2,1)}, ...), branch_computations={%region_7.8_spmd, %region_8.9_spmd} | conditional | flops 6526599168 | bytes 183517216 | solution.py:219
  532.8 27.9 %fusion.72 = f32[16,256,4096]{2,1,0:T(8,128)} fusion(bf16[256,16,64]{0,2,1:T(8,128)(2,1)S(1)} %get-tuple-element.87, bf16[4096,16,64]{0,2,1:T(8,128)(2,1)} %bitcast.149), kind=kOutput, calls=%fused_computation.131 | convolution fusion | flops 2147483648 | bytes 76021760 | tf_op jit(solution)/shard_map/cond/branch_1_fun/qhd,khd->hqk/dot_general | solution.py:206
  560.7 12.0 %copy.47 = bf16[4096,1024]{0,1:T(8,128)(2,1)} copy(bf16[4096,1024]{1,0:T(8,128)(2,1)} %get-tuple-element.88) | data formatting | bytes 16777216 | tf_op jit(solution)/shard_map
  572.7 35.8 %fusion.12 = f32[256,16,64]{0,2,1:T(8,128)S(1)} fusion(bf16[4096,16,64]{0,2,1:T(8,128)(2,1)} %bitcast.150, f32[16,256,4096]{2,1,0:T(8,128)} %fusion.72, bf16[256,16,64]{0,2,1:T(8,128)(2,1)} %get-tuple-element.89, bf16[4096,16,64]{0,2,1:T(8,128)(2,1)} %bitcast.156, f32[16,256]{1,0:T(8,128)S(1)} %get-tuple-element.49, pred[256,4096]{1,0:T(8,128)(4,1)S(1)} %copy-done.16), kind=kOutput, calls=%fused_computation.13 | convolution fusion | flops 4379115520 | bytes 86523904 | tf_op jit(solution)/shard_map/cond/branch_1_fun/hqk,khd->qhd/dot_general | solution.py:215
  608.6 1.0 split.24
  609.5 19.2 %all_gather.36 = f32[16,4096]{1,0:T(8,128)S(1)} all-gather(f32[16,256]{1,0:T(8,128)S(1)} %bitcast_divide_fusion.1), channel_id=1, replica_groups=mesh['ctx'=16,'fsdp'=2] {'ctx'}, dimensions={1}, use_global_device_ids=true | all-gather | bytes 278528 | tf_op jit(solution)/shard_map/all_gather | solution.py:225
  628.8 13.2 %all-gather.20.cloned.1.call-done = bf16[4096,1024]{0,1:T(8,128)(2,1)} async-done(((bf16[256,1024]{0,1:T(8,128)(2,1)}), bf16[4096,1024]{0,1:T(8,128)(2,1)}) %all-gather.20.cloned.1.call-update) | async-done | bytes 8388624 | tf_op jit(solution)/shard_map/all_gather | solution.py:230
  642.0 89.5 %conditional.5 = (f32[256,16,64]{0,2,1:T(8,128)S(1)}, bf16[256,1024]{0,1:T(8,128)(2,1)}) conditional(s32[]{:T(128)} %convert_element_type.134, () %tuple.36, (pred[4096,256]{1,0:T(8,128)(4,1)}, bf16[4096,1024]{0,1:T(8,128)(2,1)}, bf16[256,16,64]{0,2,1:T(8,128)(2,1)S(1)}, bf16[4096,1024]{0,1:T(8,128)(2,1)}, bf16[256,1024]{1,0:T(8,128)(2,1)S(1)}, ...), branch_computations={%region_10.11_spmd, %region_11.12_spmd} | conditional | flops 8724676608 | bytes 240910352 | solution.py:259
  642.2 28.4 %fusion.73 = f32[16,4096,256]{2,1,0:T(8,128)} fusion(bf16[4096,16,64]{0,2,1:T(8,128)(2,1)} %bitcast.146, bf16[256,16,64]{0,2,1:T(8,128)(2,1)S(1)} %get-tuple-element.52), kind=kOutput, calls=%fused_computation.132 | convolution fusion | flops 2147483648 | bytes 76021760 | tf_op jit(solution)/shard_map/cond/branch_1_fun/qhd,khd->hqk/dot_general | solution.py:239
  670.8 33.0 %fusion.21 = f32[256,16,64]{0,2,1:T(8,128)S(1)} fusion(bf16[4096,16,64]{0,2,1:T(8,128)(2,1)} %bitcast.147, f32[16,4096,256]{2,1,0:T(8,128)} %fusion.73, bf16[4096,16,64]{0,2,1:T(8,128)(2,1)} %bitcast.180, bf16[256,16,64]{0,2,1:T(8,128)(2,1)S(1)} %bitcast.173, f32[16,4096]{1,0:T(8,128)S(1)} %get-tuple-element.55, pred[4096,256]{1,0:T(8,128)(4,1)} %get-tuple-element.50), kind=kOutput, calls=%fused_computation.23 | convolution fusion | flops 4379115520 | bytes 86769664 | tf_op jit(solution)/shard_map/cond/branch_1_fun/hqk,qhd->khd/dot_general | solution.py:248
  703.8 27.6 %fusion.22 = bf16[16,256,64]{1,2,0:T(8,128)(2,1)} fusion(bf16[4096,16,64]{0,2,1:T(8,128)(2,1)} %bitcast.181, f32[16,4096,256]{2,1,0:T(8,128)} %fusion.73, pred[4096,256]{1,0:T(8,128)(4,1)} %get-tuple-element.50), kind=kOutput, calls=%fused_computation.24 | convolution fusion | flops 2198077440 | bytes 77070336 | tf_op jit(solution)/shard_map/cond/branch_1_fun/hqk,qhd->khd/dot_general | solution.py:251
  731.6 1.3 add_convert_fusion.1
  733.0 3.3 convolution_convert_fusion.2
  736.6 10.3 pad_maximum_fusion
  747.1 19.2 %reduce-scatter.5.cloned.1.call-done = bf16[2560,1024]{1,0:T(8,128)(2,1)} async-done(((bf16[5120,1024]{1,0:T(8,128)(2,1)}), bf16[2560,1024]{1,0:T(8,128)(2,1)}) %reduce-scatter.5.cloned.1.call-update) | async-done | bytes 5242896 | tf_op jit(solution)/shard_map/reduce_scatter | solution.py:289
  766.4 169.4 %reduce-scatter.3.cloned.1.call-done = bf16[512,7168]{1,0:T(8,128)(2,1)} async-done(((bf16[1024,7168]{1,0:T(8,128)(2,1)}), bf16[512,7168]{1,0:T(8,128)(2,1)}) %reduce-scatter.3.cloned.1.call-update) | async-done | bytes 7340048 | tf_op jit(solution)/shard_map/reduce_scatter | solution.py:280
  935.8 0.7 copy-done.38
  936.5 6.5 fusion.74
  943.1 8.6 fusion.44
  951.7 1.5 convert_reduce_fusion.1
  953.3 3.1 fusion.66
  957.0 1.3 convert_reduce_fusion.2
  958.3 40.7 %all-reduce.6 = (f32[3072]{0:T(1024)}, f32[4096]{0:T(1024)}, f32[1024]{0:T(1024)S(1)}, f32[1024]{0:T(1024)}, f32[1024]{0:T(1024)}) all-reduce(f32[3072]{0:T(1024)S(1)} %convert_reduce_fusion.1, f32[4096]{0:T(1024)S(1)} %copy-done.30, f32[1024]{0:T(1024)S(1)} %get-tuple-element.134, ...), channel_id=1, replica_groups=mesh['ctx'=16,'fsdp'=2] {'ctx','fsdp'}, use_global_device_ids=true, to_apply=%region_19.20 | all-reduce | flops 10240 | bytes 81920 | tf_op jit(solution)/shard_map/psum | solution.py:299
  999.0 173.6 %all-reduce.10.cloned.1.call-done = (bf16[512,7168]{1,0:T(8,128)(2,1)}, bf16[2560,1024]{1,0:T(8,128)(2,1)}) async-done(((bf16[512,7168]{1,0:T(8,128)(2,1)}, bf16[2560,1024]{1,0:T(8,128)(2,1)}), (bf16[512,7168]{1,0:T(8,128)(2,1)}, bf16[2560,1024]{1,0:T(8,128)(2,1)})) %all-reduce.10.cloned.1.call-update) | async-done | bytes 12582928 | tf_op jit(solution)/shard_map/psum | solution.py:296
  1172.6 7.7 slice.76
  1180.3 3.5 slice.75
  1183.8 4.4 slice.78
  1188.3 1.6 slice.77
  1189.8 0.6 copy.68
  (143 shorter events, 6.9 us)
Async XLA Ops:
  7.2 7.0 copy-start
  7.2 83.8 %all-gather.8.cloned.1.call-start = ((), (), s32[]{:S(2)}) async-start(), calls=%async_computation.2 | async-start | bytes 9437184 | tf_op jit(solution)/shard_map/all_gather | solution.py:106
  7.9 214.7 %all-gather.16.cloned.1.call-start = ((), (), s32[]{:S(2)}) async-start(), calls=%async_computation.6 | async-start | bytes 15728640 | tf_op jit(solution)/shard_map/all_gather | solution.py:180
  13.4 0.7 copy-start.36
  13.4 0.7 copy-start.37
  13.4 0.7 copy-start.34
  13.4 0.7 copy-start.40
  13.4 1.4 copy-start.4
  13.4 288.6 %all-gather.10.cloned.1.call-start = ((), (), s32[]{:S(2)}) async-start(), calls=%async_computation.3 | async-start | bytes 8912896 | tf_op jit(solution)/shard_map/all_gather | solution.py:138
  14.1 511.1 %copy-start.18 = (f32[1024]{0:T(1024)}, f32[1024]{0:T(1024)S(1)}, u32[]{:S(2)}) copy-start(f32[1024]{0:T(1024)S(1)} %convert_element_type.117) | copy-start | bytes 12292
  14.1 511.1 %copy-start.20 = (f32[1024]{0:T(1024)}, f32[1024]{0:T(1024)S(1)}, u32[]{:S(2)}) copy-start(f32[1024]{0:T(1024)S(1)} %convert_element_type.118) | copy-start | bytes 12292
  15.0 510.2 %copy-start.26 = (f32[256]{0:T(256)}, f32[256]{0:T(256)S(1)}, u32[]{:S(2)}) copy-start(f32[256]{0:T(256)S(1)} %broadcast_multiply_fusion) | copy-start | bytes 3076
  15.3 80.4 %copy-start.31 = (f32[256]{0:T(256)}, f32[256]{0:T(256)S(1)}, u32[]{:S(2)}) copy-start(f32[256]{0:T(256)S(1)} %fusion.50) | copy-start | bytes 3076
  15.3 509.9 %copy-start.28 = (f32[256]{0:T(256)}, f32[256]{0:T(256)S(1)}, u32[]{:S(2)}) copy-start(f32[256]{0:T(256)S(1)} %fusion.59) | copy-start | bytes 3076
  15.4 85.0 %copy-start.22 = (f32[256,8]{0,1:T(8,128)}, f32[256,8]{0,1:T(8,128)S(1)}, u32[]{:S(2)}) copy-start(f32[256,8]{0,1:T(8,128)S(1)} %get-tuple-element.142) | copy-start | bytes 24580
  15.5 85.0 %copy-start.24 = (f32[256,8]{0,1:T(8,128)}, f32[256,8]{0,1:T(8,128)S(1)}, u32[]{:S(2)}) copy-start(f32[256,8]{0,1:T(8,128)S(1)} %get-tuple-element.143) | copy-start | bytes 24580
  95.7 1.7 copy-start.12
  102.5 4.1 copy-start.17
  102.5 274.8 %all-gather.12.cloned.1.call-start = ((), (), s32[]{:S(2)}) async-start(), calls=%async_computation.4 | async-start | bytes 8912896 | tf_op jit(solution)/shard_map/all_gather | solution.py:139
  104.9 117.7 %copy-start.13 = (bf16[1,256,1024]{2,1,0:T(8,128)(2,1)S(1)}, bf16[1,256,1024]{2,1,0:T(8,128)(2,1)}, u32[]{:S(2)}) copy-start(bf16[1,256,1024]{2,1,0:T(8,128)(2,1)} %param.22) | copy-start | bytes 1572868
  104.9 377.4 %all-gather.14.cloned.1.call-start = ((), (), s32[]{:S(2)}) async-start(), calls=%async_computation.5 | async-start | bytes 12582912 | tf_op jit(solution)/shard_map/all_gather | solution.py:107
  105.5 523.3 %all-gather.18.cloned.1.call-start = ((), (), s32[]{:S(2)}) async-start(), calls=%async_computation.7 | async-start | bytes 8912896 | tf_op jit(solution)/shard_map/all_gather | solution.py:229
  106.5 535.4 %all-gather.20.cloned.1.call-start = ((), (), s32[]{:S(2)}) async-start(), calls=%async_computation.8 | async-start | bytes 8912896 | tf_op jit(solution)/shard_map/all_gather | solution.py:230
  111.2 266.1 %copy-start.9 = (bf16[256,16,64]{0,2,1:T(8,128)(2,1)S(1)}, bf16[256,16,64]{0,2,1:T(8,128)(2,1)}, u32[]{:S(2)}) copy-start(bf16[256,16,64]{0,2,1:T(8,128)(2,1)} %maximum_convert_fusion.1) | copy-start | bytes 1572868
  228.6 2.4 copy-start.10
  377.3 71.9 %copy-start.33 = (bf16[4096]{0:T(1024)(128)(2,1)S(1)}, bf16[4096]{0:T(1024)(128)(2,1)}, u32[]{:S(2)}) copy-start(bf16[4096]{0:T(1024)(128)(2,1)} %param.28) | copy-start | bytes 24580
  448.9 317.5 %reduce-scatter.5.cloned.1.call-start = ((), (), s32[]{:S(2)}) async-start(), calls=%async_computation.10 | async-start | bytes 15728640 | tf_op jit(solution)/shard_map/reduce_scatter | solution.py:289
  507.4 5.9 copy-start.14
  511.8 1.5 copy-start.6
  518.8 417.0 %reduce-scatter.3.cloned.1.call-start = ((), (), s32[]{:S(2)}) async-start(), calls=%async_computation.9 | async-start | bytes 22020096 | tf_op jit(solution)/shard_map/reduce_scatter | solution.py:280
  532.8 109.1 %copy-start.8 = (bf16[256,16,64]{0,2,1:T(8,128)(2,1)S(1)}, bf16[256,16,64]{0,2,1:T(8,128)(2,1)}, u32[]{:S(2)}) copy-start(bf16[256,16,64]{0,2,1:T(8,128)(2,1)} %maximum_convert_fusion) | copy-start | bytes 1572868
  532.8 109.1 %copy-start.11 = (bf16[256,1024]{1,0:T(8,128)(2,1)S(1)}, bf16[256,1024]{1,0:T(8,128)(2,1)}, u32[]{:S(2)}) copy-start(bf16[256,1024]{1,0:T(8,128)(2,1)} %slice.93) | copy-start | bytes 1572868
  560.7 12.0 %copy-start.16 = (pred[256,4096]{1,0:T(8,128)(4,1)S(1)}, pred[256,4096]{1,0:T(8,128)(4,1)}, u32[]{:S(2)}) copy-start(pred[256,4096]{1,0:T(8,128)(4,1)} %get-tuple-element.44) | copy-start | bytes 3145732 | tf_op jit(solution)/shard_map/cond
  642.0 89.6 %copy-start.23 = (f32[256,8]{0,1:T(8,128)S(1)}, f32[256,8]{0,1:T(8,128)}, u32[]{:S(2)}) copy-start(f32[256,8]{0,1:T(8,128)} %copy-done.22) | copy-start | bytes 24580
  642.0 89.6 %copy-start.25 = (f32[256,8]{0,1:T(8,128)S(1)}, f32[256,8]{0,1:T(8,128)}, u32[]{:S(2)}) copy-start(f32[256,8]{0,1:T(8,128)} %copy-done.24) | copy-start | bytes 24580
  731.4 1.5 copy-start.5
  731.4 1.5 copy-start.19
  731.4 1.6 copy-start.21
  731.4 1.6 copy-start.27
  731.5 1.6 copy-start.29
  733.0 3.5 copy-start.2
  746.9 425.7 %all-reduce.10.cloned.1.call-start = ((), (), s32[]{:S(2)}) async-start(), calls=%async_computation.11 | async-start | bytes 25165824 | tf_op jit(solution)/shard_map/psum | solution.py:296
  935.8 0.7 copy-start.38
  935.8 0.7 copy-start.39
  936.5 6.5 copy-start.7
  936.5 16.7 %slice-start.2 = ((s8[6291456]{0:T(1024)(128)(4,1)}), s8[4194304]{0:T(1024)(128)(4,1)S(1)}, s32[]{:S(2)}) async-start(s8[6291456]{0:T(1024)(128)(4,1)} %bitcast.182), calls=%async_computation.14 | async-start | bytes 8388608
  943.1 10.2 slice-start.3
  953.2 3.2 copy-start.32
  953.3 3.8 copy-start.15
  956.4 1.9 copy-start.30
  999.0 190.9 %copy-start.35 = (f32[1024]{0:T(1024)}, f32[1024]{0:T(1024)S(1)}, u32[]{:S(2)}) copy-start(f32[1024]{0:T(1024)S(1)} %get-tuple-element.177) | copy-start | bytes 12292
  1172.6 11.2 slice-start
  1172.6 7.7 copy-start.3
  1172.6 11.2 slice-start.1
  1183.8 6.6 copy-start.1
Sparse Core Ops, SparseCore 0:
  9.6 81.3 all-gather.7
  93.1 129.5 all-gather.15
  225.4 76.6 all-gather.9
  304.0 73.1 all-gather.11
  378.7 103.6 all-gather.13
  484.9 76.6 all-gather.17
  563.7 78.1 all-gather.19
  644.2 122.1 reduce-scatter.4
  768.7 167.0 reduce-scatter.2
  939.7 232.8 all-reduce.9
where the time goes:
time: 1210 us; the launch traced here: 1200 us
  waiting for transfers between devices  733 us (61%)
  matrix products  273 us (23%)
  local copies, waits for them, and re-layouts  73.2 us (6%)
  blocking collectives  59.9 us (5%)
  other arithmetic  40.8 us (3%)
  between operations  16.3 us (1%)
    psum x1, waiting for transfers between devices, local(): lax.psum(in_share, 'ctx').astype(jnp.float32)  174 us
    reduce_scatter x1, waiting for transfers between devices, local(): lax.psum_scatter(jnp.concatenate([contract_first(columns, grad_merged), c...  169 us
    all_gather x1, waiting for transfers between devices, local(): lax.all_gather(local_out, 'fsdp', axis=0, tiled=True)  111 us
    all_gather x1, waiting for transfers between devices, local(): lax.all_gather(w_qkv, 'fsdp', axis=0, tiled=True)  75.5 us
    all_gather x1, waiting for transfers between devices, local(): lax.all_gather(values_flat, 'ctx', axis=0, tiled=True)  75.2 us
    all_gather x1, waiting for transfers between devices, local(): lax.all_gather(keys_flat, 'ctx', axis=0, tiled=True)  71 us
    psum x1, blocking collectives, local(): lax.psum((jnp.sum(grad_merged, axis=0, dtype=jnp.float32), jnp.sum(grad_u...  40.7 us
    dot_general x1, matrix products, query_compute(): jnp.einsum('hqk,khd->qhd', slopes, keys_piece, preferred_element_type=jnp...  35.8 us
  transfers between devices with their start and end apart: 10, of which 9 were waited for; matrix products, arithmetic and copies ran while one was open for 30% of the time, Pallas kernels for 0%

commit v1 on v0

v1 whole, which is shorter than its diff:
```python
import functools
import math

import jax
import jax.numpy as jnp
from jax import lax
from jax.experimental import pallas as pl
from jax.experimental.pallas import tpu as pltpu
from jax.sharding import PartitionSpec as P

D = 1024
HEADS = 16
HDIM = 64
FF = 4096
ROT = 16
CLEN = 1024
EPS = 1e-05
LANES = 128
MESH = pl.DeviceIdType.MESH
F32 = jnp.float32
BF16 = jnp.bfloat16
VMEM_SPEC = pl.BlockSpec(memory_space=pltpu.VMEM)
ANY_SPEC = pl.BlockSpec(memory_space=pl.ANY)
SCALE = HDIM**-0.5
LOG2E = math.log2(math.e)


def dot(a, b, ca=1, cb=0):
    return lax.dot_general(a, b, (((ca,), (cb,)), ((), ())), preferred_element_type=F32)


def guarded(cond, act):
    if cond is None:
        act()
    else:
        pl.when(cond)(act)


def greet(partners):
    barrier = pltpu.get_barrier_semaphore()
    for cond, device in partners:

        def signal(device=device):
            pl.semaphore_signal(barrier, inc=1, device_id=device, device_id_type=MESH)

        guarded(cond, signal)
    expected = sum(1 if cond is None else cond.astype(jnp.int32) for cond, _ in partners)
    pl.semaphore_wait(barrier, expected)


class Place:
    def __init__(self, count):
        self.depth = count // 4
        self.me = lax.axis_index("ctx")
        self.core = lax.rem(self.me, 2)
        self.x = lax.rem(lax.div(self.me, 2), 2)
        self.z = lax.div(self.me, 4)
        self.sibling = self.me + 1 - 2 * self.core
        self.across = self.me + 2 - 4 * self.x
        self.above = self.me + 4
        self.below = self.me - 4
        self.has_above = self.z < self.depth - 1
        self.has_below = self.z > 0

    def partners(self):
        return [
            (None, {"ctx": self.sibling}),
            (None, {"ctx": self.across}),
            (self.has_above, {"ctx": self.above}),
            (self.has_below, {"ctx": self.below}),
        ]

    def index(self, x, z, core):
        return (z * 2 + x) * 2 + core


def fsdp_peers(shards):
    mine = lax.axis_index("fsdp")
    return mine, [lax.rem(mine + k, shards) for k in range(1, shards)]


class Gather:
    def __init__(self, place, sources, outs, send, recv):
        self.place, self.sources, self.outs = place, sources, outs
        self.send, self.recv = send, recv
        self.started = []
        self.slot = 0

    def copies(self, shard, device, slot, own):
        for a, (source, out) in enumerate(zip(self.sources, self.outs)):
            yield pltpu.make_async_remote_copy(
                src_ref=source if own else out.at[shard],
                dst_ref=out.at[shard],
                send_sem=self.send.at[a, slot],
                recv_sem=self.recv.at[a, shard],
                device_id={"ctx": device},
                device_id_type=MESH,
            )

    def start(self, cond, shard, device, own=False):
        slot = self.slot
        self.slot += 1

        def act():
            for copy in self.copies(shard, device, slot, own):
                copy.start()

        guarded(cond, act)
        self.started.append((cond, shard, device, slot, own))

    def arrived(self, shard):
        for copy in self.copies(shard, self.place.sibling, 0, False):
            copy.wait_recv()

    def column(self, z, cond):
        shard = self.place.index(1 - self.place.x, z, self.place.core)
        guarded(cond, lambda: self.arrived(shard))
        self.start(cond, shard, self.place.sibling)

    def run(self):
        p = self.place
        own = p.me
        self.start(p.has_above, own, p.above, True)
        self.start(p.has_below, own, p.below, True)
        self.start(None, own, p.across, True)
        self.start(None, own, p.sibling, True)
        for step in range(1, p.depth):
            for sign in (1, -1):
                z = p.z - sign * step
                here = z >= 0 if sign == 1 else z < p.depth
                onward = jnp.logical_and(here, p.has_above if sign == 1 else p.has_below)
                shard = p.index(p.x, z, p.core)
                guarded(here, lambda shard=shard: self.arrived(shard))
                self.start(onward, shard, p.above if sign == 1 else p.below)
                self.start(here, shard, p.across)
                self.start(here, shard, p.sibling)
            self.columns(step - 1)
        self.columns(p.depth - 1)

    def columns(self, step):
        p = self.place
        if step == 0:
            self.column(p.z, None)
            return
        for sign in (1, -1):
            z = p.z - sign * step
            self.column(z, z >= 0 if sign == 1 else z < p.depth)

    def finish(self):
        p = self.place
        for z in range(p.depth):
            for x in range(2):
                self.arrived(p.index(x, z, 1 - p.core))
        for cond, shard, device, slot, own in self.started:

            def act(shard=shard, device=device, slot=slot, own=own):
                for copy in self.copies(shard, device, slot, own):
                    copy.wait_send()

            guarded(cond, act)


def gather_sems(count, arrays):
    depth = count // 4
    sends = 4 + 6 * (depth - 1) + 2 * depth
    return [pltpu.SemaphoreType.DMA((arrays, sends)), pltpu.SemaphoreType.DMA((arrays, count))]


def gather_kernel(count, x_ref, o_ref, send, recv, keep_sem):
    place = Place(count)
    greet(place.partners())
    keep = pltpu.make_async_copy(x_ref, o_ref.at[place.me], keep_sem)
    keep.start()
    ring = Gather(place, [x_ref], [o_ref], send, recv)
    ring.run()
    ring.finish()
    keep.wait()


def gather(x, count, collective_id):
    return pl.pallas_call(
        functools.partial(gather_kernel, count),
        out_shape=jax.ShapeDtypeStruct((count,) + x.shape, x.dtype),
        in_specs=[VMEM_SPEC],
        out_specs=ANY_SPEC,
        scratch_shapes=gather_sems(count, 1) + [pltpu.SemaphoreType.DMA],
        compiler_params=pltpu.CompilerParams(collective_id=collective_id, has_side_effects=True),
        name="gather",
    )(x)


def first_kernel(count, shards, x_ref, a_ref, b_ref, o_ref, ao_ref, bo_ref, send, recv, fsend, frecv, keep_sem):
    place = Place(count)
    mine, peers = fsdp_peers(shards)
    greet(place.partners() + [(None, {"fsdp": peer}) for peer in peers])
    keeps = [
        pltpu.make_async_copy(x_ref, o_ref.at[place.me], keep_sem.at[0]),
        pltpu.make_async_copy(a_ref, ao_ref.at[mine], keep_sem.at[1]),
        pltpu.make_async_copy(b_ref, bo_ref.at[mine], keep_sem.at[2]),
    ]
    moves = []
    for k, peer in enumerate(peers):
        for a, (source, out) in enumerate(((a_ref, ao_ref), (b_ref, bo_ref))):
            moves.append(
                pltpu.make_async_remote_copy(
                    src_ref=source,
                    dst_ref=out.at[mine],
                    send_sem=fsend.at[a, k],
                    recv_sem=frecv.at[a, k],
                    device_id={"fsdp": peer},
                    device_id_type=MESH,
                )
            )
    for move in moves + keeps:
        move.start()
    ring = Gather(place, [x_ref], [o_ref], send, recv)
    ring.run()
    ring.finish()
    for move in moves + keeps:
        move.wait()


def first_exchange(x, a, b, count, shards):
    return pl.pallas_call(
        functools.partial(first_kernel, count, shards),
        out_shape=[
            jax.ShapeDtypeStruct((count,) + x.shape, x.dtype),
            jax.ShapeDtypeStruct((shards,) + a.shape, a.dtype),
            jax.ShapeDtypeStruct((shards,) + b.shape, b.dtype),
        ],
        in_specs=[VMEM_SPEC] * 3,
        out_specs=[ANY_SPEC] * 3,
        scratch_shapes=gather_sems(count, 1)
        + [pltpu.SemaphoreType.DMA((2, shards - 1))] * 2
        + [pltpu.SemaphoreType.DMA((3,))],
        compiler_params=pltpu.CompilerParams(collective_id=0, has_side_effects=True),
        name="first_exchange",
    )(x, a, b)


def add_rows(out, terms, rows, step=32):
    def body(i, carry):
        at = pl.ds(pl.multiple_of(i * step, step), step)
        total = terms[0][at, :].astype(F32)
        for term in terms[1:]:
            total = total + term[at, :].astype(F32)
        out[at, :] = total.astype(out.dtype)
        return carry

    lax.fori_loop(0, rows // step, body, 0)


def scatter_kernel(count, p_ref, o_ref, held, pair, side, upward, downward, load, ssend, srecv, xsend, xrecv, zsend, urecv, drecv):
    place = Place(count)
    depth, rows = place.depth, o_ref.shape[0]
    greet(place.partners())

    def slot(x, z):
        return x * depth + z

    def loading(x, z):
        s = slot(x, z)
        return pltpu.make_async_copy(p_ref.at[place.index(x, z, place.core)], held.at[s], load.at[s])

    def pairing(x, z):
        s = slot(x, z)
        return pltpu.make_async_remote_copy(
            src_ref=p_ref.at[place.index(x, z, 1 - place.core)],
            dst_ref=pair.at[s],
            send_sem=ssend.at[s],
            recv_sem=srecv.at[s],
            device_id={"ctx": place.sibling},
            device_id_type=MESH,
        )

    def crossing(z):
        return pltpu.make_async_remote_copy(
            src_ref=held.at[slot(1 - place.x, z)],
            dst_ref=side.at[z],
            send_sem=xsend.at[z],
            recv_sem=xrecv.at[z],
            device_id={"ctx": place.across},
            device_id_type=MESH,
        )

    def rising(z):
        return pltpu.make_async_remote_copy(
            src_ref=held.at[slot(place.x, z)],
            dst_ref=upward.at[z],
            send_sem=zsend.at[z],
            recv_sem=urecv.at[z],
            device_id={"ctx": place.above},
            device_id_type=MESH,
        )

    def falling(z):
        return pltpu.make_async_remote_copy(
            src_ref=held.at[slot(place.x, z)],
            dst_ref=downward.at[z],
            send_sem=zsend.at[z],
            recv_sem=drecv.at[z],
            device_id={"ctx": place.below},
            device_id_type=MESH,
        )

    order = []
    for step in range(depth - 1, 0, -1):
        for sign in (1, -1):
            z = place.z + sign * step
            order.append((z, z < depth if sign == 1 else z >= 0, sign))
    order.append((place.z, None, 0))

    for z, cond, _ in order:

        def begin(z=z):
            for x in (1 - place.x, place.x):
                pairing(x, z).start()
                loading(x, z).start()

        guarded(cond, begin)

    def pair_up(z):
        for x in (1 - place.x, place.x):
            s = slot(x, z)
            loading(x, z).wait()
            pairing(x, z).wait_recv()
            add_rows(held.at[s], [held.at[s], pair.at[s]], rows)
            if x is not place.x:
                crossing(z).start()

    def pass_on(z, sign):
        mine = held.at[slot(place.x, z)]
        crossing(z).wait_recv()
        if sign == 1:

            @pl.when(place.has_below)
            def _():
                rising(z).wait_recv()
                add_rows(mine, [mine, side.at[z], upward.at[z]], rows)

            @pl.when(jnp.logical_not(place.has_below))
            def _():
                add_rows(mine, [mine, side.at[z]], rows)

            rising(z).start()
        else:

            @pl.when(place.has_above)
            def _():
                falling(z).wait_recv()
                add_rows(mine, [mine, side.at[z], downward.at[z]], rows)

            @pl.when(jnp.logical_not(place.has_above))
            def _():
                add_rows(mine, [mine, side.at[z]], rows)

            falling(z).start()

    def settle():
        z = place.z
        mine = held.at[slot(place.x, z)]
        crossing(z).wait_recv()
        inner = jnp.logical_and(place.has_below, place.has_above)

        @pl.when(place.has_below)
        def _():
            rising(z).wait_recv()

        @pl.when(place.has_above)
        def _():
            falling(z).wait_recv()

        @pl.when(inner)
        def _():
            add_rows(o_ref, [mine, side.at[z], upward.at[z], downward.at[z]], rows)

        @pl.when(jnp.logical_not(place.has_above))
        def _():
            add_rows(o_ref, [mine, side.at[z], upward.at[z]], rows)

        @pl.when(jnp.logical_not(place.has_below))
        def _():
            add_rows(o_ref, [mine, side.at[z], downward.at[z]], rows)

    for i, (z, cond, _) in enumerate(order):
        guarded(cond, lambda z=z: pair_up(z))
        if i:
            back, back_cond, back_sign = order[i - 1]
            guarded(back_cond, lambda: pass_on(back, back_sign))
    settle()

    for z, cond, sign in order:

        def end(z=z, sign=sign):
            for x in (1 - place.x, place.x):
                pairing(x, z).wait_send()
            crossing(z).wait_send()
            if sign == 1:
                rising(z).wait_send()
            elif sign == -1:
                falling(z).wait_send()

        guarded(cond, end)


def scatter(partial, count, collective_id):
    _, rows, cols = partial.shape
    depth = count // 4
    dma = pltpu.SemaphoreType.DMA
    return pl.pallas_call(
        functools.partial(scatter_kernel, count),
        out_shape=jax.ShapeDtypeStruct((rows, cols), F32),
        in_specs=[ANY_SPEC],
        out_specs=VMEM_SPEC,
        scratch_shapes=[pltpu.VMEM((2 * depth, rows, cols), BF16)] * 2
        + [pltpu.VMEM((depth, rows, cols), BF16)] * 3
        + [dma((2 * depth,))] * 3
        + [dma((depth,))] * 5,
        compiler_params=pltpu.CompilerParams(collective_id=collective_id, has_side_effects=True),
        name="scatter",
    )(partial)


def grads_kernel(count, shards, a_ref, b_ref, ao_ref, bo_ref, a_in, b_in, a_sum, b_sum, send, recv, fsend, frecv, keep_sem):
    place = Place(count)
    mine, peers = fsdp_peers(shards)
    greet(place.partners() + [(None, {"fsdp": peer}) for peer in peers])
    moves = []
    for k, peer in enumerate(peers):
        for a, (source, landing) in enumerate(((a_ref, a_in), (b_ref, b_in))):
            moves.append(
                pltpu.make_async_remote_copy(
                    src_ref=source.at[peer],
                    dst_ref=landing.at[k],
                    send_sem=fsend.at[a, k],
                    recv_sem=frecv.at[a, k],
                    device_id={"fsdp": peer},
                    device_id_type=MESH,
                )
            )
    for move in moves:
        move.start()
    for move in moves:
        move.wait_recv()
    for source, landing, total in ((a_ref, a_in, a_sum), (b_ref, b_in, b_sum)):
        terms = [source.at[mine]] + [landing.at[k] for k in range(shards - 1)]
        add_rows(total, terms, total.shape[0], 16)
    keeps = [
        pltpu.make_async_copy(a_sum, ao_ref.at[place.me], keep_sem.at[0]),
        pltpu.make_async_copy(b_sum, bo_ref.at[place.me], keep_sem.at[1]),
    ]
    for keep in keeps:
        keep.start()
    ring = Gather(place, [a_sum, b_sum], [ao_ref, bo_ref], send, recv)
    ring.run()
    ring.finish()
    for move in moves:
        move.wait_send()
    for keep in keeps:
        keep.wait()


def grads_exchange(a, b, count, shards, collective_id):
    dma = pltpu.SemaphoreType.DMA
    return pl.pallas_call(
        functools.partial(grads_kernel, count, shards),
        out_shape=[
            jax.ShapeDtypeStruct((count,) + a.shape[1:], a.dtype),
            jax.ShapeDtypeStruct((count,) + b.shape[1:], b.dtype),
        ],
        in_specs=[VMEM_SPEC] * 2,
        out_specs=[ANY_SPEC] * 2,
        scratch_shapes=[
            pltpu.VMEM((shards - 1,) + a.shape[1:], a.dtype),
            pltpu.VMEM((shards - 1,) + b.shape[1:], b.dtype),
            pltpu.VMEM(a.shape[1:], a.dtype),
            pltpu.VMEM(b.shape[1:], b.dtype),
        ]
        + gather_sems(count, 2)
        + [dma((2, shards - 1))] * 2
        + [dma((2,))],
        compiler_params=pltpu.CompilerParams(collective_id=collective_id, has_side_effects=True),
        name="grads_exchange",
    )(a, b)


def turn(values, cos, sin):
    lane = lax.broadcasted_iota(jnp.int32, values.shape, 1) % HDIM
    half = ROT // 2
    other = jnp.where(lane < half, pltpu.roll(values, LANES - half, 1), pltpu.roll(values, half, 1))
    return values * cos + other * sin


def project_kernel(x_ref, w_ref, b_ref, cos_ref, sin_ref, o_ref):
    merged = dot(x_ref[0], w_ref[...]) + b_ref[...]
    o_ref[:, :LANES] = turn(merged[:, :LANES], cos_ref[...], sin_ref[...]).astype(BF16)
    o_ref[:, LANES:] = merged[:, LANES:].astype(BF16)


def project(gathered, w, b, cos, sin):
    count, rows, _ = gathered.shape
    return pl.pallas_call(
        project_kernel,
        grid=(count,),
        out_shape=jax.ShapeDtypeStruct((count * rows, 2 * LANES), BF16),
        in_specs=[
            pl.BlockSpec((1, rows, D), lambda i: (i, 0, 0)),
            pl.BlockSpec(w.shape, lambda i: (0, 0)),
            pl.BlockSpec(b.shape, lambda i: (0, 0)),
            pl.BlockSpec((rows, LANES), lambda i: (i, 0)),
            pl.BlockSpec((rows, LANES), lambda i: (i, 0)),
        ],
        out_specs=pl.BlockSpec((rows, 2 * LANES), lambda i: (i, 0)),
        name="project",
    )(gathered, w, b, cos, sin)


TILE = 512


def below_diagonal(transposed=False):
    row = lax.broadcasted_iota(jnp.int32, (TILE, TILE), 0)
    col = lax.broadcasted_iota(jnp.int32, (TILE, TILE), 1)
    return row <= col if transposed else col <= row


def attend_kernel(tokens, block, order_ref, x_ref, o_ref, q_s, k_s, v_s):
    low = lax.broadcasted_iota(jnp.int32, (block, LANES), 1) < HDIM

    def fetch(j, carry):
        source = pl.ds(pl.multiple_of(order_ref[j] * block, block), block)
        target = pl.ds(pl.multiple_of(j * block, block), block)
        qk = x_ref[source, :LANES].astype(F32)
        q_s[target, :] = jnp.where(low, qk, 0.0).astype(BF16)
        k_s[target, :] = jnp.where(low, pltpu.roll(qk, HDIM, 1), 0.0).astype(BF16)
        v_s[target, :] = x_ref[source, LANES:]
        return carry

    lax.fori_loop(0, tokens // block, fetch, 0)
    prompt = tokens // 2
    per_run = CLEN // TILE

    def step(queries, key_tile, total, masked=False):
        at = pl.ds(pl.multiple_of(key_tile * TILE, TILE), TILE)
        weights = jnp.exp2(dot(queries, k_s[at, :], 1, 1) * (SCALE * LOG2E))
        if masked:
            weights = jnp.where(below_diagonal(), weights, 0.0)
        return total + dot(weights.astype(BF16), v_s[at, :])

    def one(tile, first, before):
        queries = q_s[pl.ds(pl.multiple_of(tile * TILE, TILE), TILE), :]
        total = step(queries, tile, jnp.zeros((TILE, LANES), F32), True)
        total = lax.fori_loop(0, before, lambda j, t: step(queries, j, t), total)
        total = lax.fori_loop(first, tile, lambda j, t: step(queries, j, t), total)
        for part in range(TILE // block):
            target = order_ref[tile * (TILE // block) + part]
            o_ref[pl.ds(pl.multiple_of(target * block, block), block), :] = total[part * block : (part + 1) * block]

    def in_prompt(tile, carry):
        one(tile, 0, 0)
        return carry

    def in_run(i, carry):
        tile = prompt // TILE + i
        one(tile, prompt // TILE + lax.div(i, per_run) * per_run, prompt // TILE)
        return carry

    lax.fori_loop(0, prompt // TILE, in_prompt, 0)
    lax.fori_loop(0, prompt // TILE, in_run, 0)


SMEM_SPEC = pl.BlockSpec(memory_space=pltpu.SMEM)


def attend(qkv, order):
    tokens = qkv.shape[0]
    block = tokens // order.shape[0]
    return pl.pallas_call(
        functools.partial(attend_kernel, tokens, block),
        out_shape=jax.ShapeDtypeStruct((tokens, LANES), F32),
        in_specs=[SMEM_SPEC, VMEM_SPEC],
        out_specs=VMEM_SPEC,
        scratch_shapes=[pltpu.VMEM((tokens, LANES), BF16)] * 3,
        name="attend",
    )(order, qkv)


def branch_kernel(
    acc_ref, x_ref, cot_ref, w_up_ref, b_up_ref, w_out_ref, keep_ref,
    out_ref, up_ref, scaled_ref, g_out_ref, g_up_ref, b_sum_ref, c_sum_ref,
):
    i = pl.program_id(0)
    units = w_up_ref.shape[1]
    acc = acc_ref[...]
    low = lax.broadcasted_iota(jnp.int32, acc.shape, 1) < HDIM
    total = jnp.where(low, pltpu.roll(acc, HDIM, 1), 1.0)
    attn = jnp.where(low, acc / total, 0.0)
    attended = (attn * keep_ref[...]).astype(BF16)
    x = x_ref[0]
    cot = cot_ref[0]
    up = dot(x, w_up_ref[...]) + b_up_ref[...]
    phi = 0.5 * (1.0 + lax.erf(up * (0.5**0.5)))
    gated = (up * phi).astype(BF16)
    slope = phi + up * jnp.exp(-0.5 * up * up) * ((2.0 * math.pi) ** -0.5)
    joined = jnp.concatenate([gated, attended], axis=1)
    out_ref[0] = dot(joined, w_out_ref[...]).astype(BF16)
    grads = dot(cot, w_out_ref[...], 1, 1)
    grad_up = (grads[:, :units] * slope).astype(BF16)
    up_ref[...] = grad_up
    grad_attn = grads[:, units:]
    scaled = jnp.where(low, grad_attn / total, 0.0)
    whole = jnp.where(low, total, 0.0)
    delta = jnp.sum(grad_attn * attn, axis=1, keepdims=True) / jnp.max(whole, axis=1, keepdims=True)
    lane = lax.broadcasted_iota(jnp.int32, acc.shape, 1)
    first = delta.astype(BF16).astype(F32)
    second = (delta - first).astype(BF16).astype(F32)
    third = delta - first - second
    scaled = jnp.where(lane == HDIM, -first, scaled)
    scaled = jnp.where(lane == HDIM + 1, -second, scaled)
    scaled = jnp.where(lane == HDIM + 2, -third, scaled)
    scaled_ref[...] = scaled.astype(BF16)
    parts = (
        (g_out_ref, dot(joined, cot, 0, 0)),
        (g_up_ref, dot(x, grad_up, 0, 0)),
        (b_sum_ref, jnp.sum(grad_up.astype(F32), axis=0, keepdims=True)),
        (c_sum_ref, jnp.sum(cot.astype(F32), axis=0, keepdims=True)),
    )

    @pl.when(i == 0)
    def _():
        for ref, value in parts:
            ref[...] = value

    @pl.when(i > 0)
    def _():
        for ref, value in parts:
            ref[...] += value


def branch(acc, gathered, cots, w_up, b_up, w_out, keep):
    count, rows, _ = gathered.shape
    tokens, units = count * rows, w_up.shape[1]
    whole = lambda shape: pl.BlockSpec(shape, lambda i: (0,) * len(shape))
    by_row = lambda cols: pl.BlockSpec((rows, cols), lambda i: (i, 0))
    by_shard = pl.BlockSpec((1, rows, D), lambda i: (i, 0, 0))
    return pl.pallas_call(
        branch_kernel,
        grid=(count,),
        out_shape=[
            jax.ShapeDtypeStruct((count, rows, D), BF16),
            jax.ShapeDtypeStruct((tokens, units), BF16),
            jax.ShapeDtypeStruct((tokens, LANES), BF16),
            jax.ShapeDtypeStruct(w_out.shape, F32),
            jax.ShapeDtypeStruct(w_up.shape, F32),
            jax.ShapeDtypeStruct((1, units), F32),
            jax.ShapeDtypeStruct((1, D), F32),
        ],
        in_specs=[
            by_row(LANES), by_shard, by_shard, whole(w_up.shape), whole(b_up.shape), whole(w_out.shape), whole(keep.shape),
        ],
        out_specs=[
            by_shard, by_row(units), by_row(LANES), whole(w_out.shape), whole(w_up.shape), whole((1, units)), whole((1, D)),
        ],
        name="branch",
    )(acc, gathered, cots, w_up, b_up, w_out, keep)


def slopes_kernel(tokens, block, order_ref, x_ref, g_ref, cos_ref, sin_ref, o_ref, q_s, k_s, r_s, v_s, g_s, dq_s):
    low = lax.broadcasted_iota(jnp.int32, (block, LANES), 1) < HDIM

    def fetch(j, carry):
        source = pl.ds(pl.multiple_of(order_ref[j] * block, block), block)
        target = pl.ds(pl.multiple_of(j * block, block), block)
        qk = x_ref[source, :LANES].astype(F32)
        rolled = pltpu.roll(qk, HDIM, 1)
        q_s[target, :] = jnp.where(low, qk, 0.0).astype(BF16)
        k_s[target, :] = jnp.where(low, rolled, 0.0).astype(BF16)
        r_s[target, :] = jnp.where(low, 0.0, rolled).astype(BF16)
        v_s[target, :] = x_ref[source, LANES:]
        g_s[target, :] = g_ref[source, :]
        dq_s[target, :] = jnp.zeros((block, LANES), F32)
        return carry

    lax.fori_loop(0, tokens // block, fetch, 0)
    prompt = tokens // 2
    per_run = CLEN // TILE

    def step(keys, values, query_tile, carry, masked=False):
        grad_k, grad_v = carry
        at = pl.ds(pl.multiple_of(query_tile * TILE, TILE), TILE)
        weights = jnp.exp2(dot(keys, q_s[at, :], 1, 1) * (SCALE * LOG2E))
        if masked:
            weights = jnp.where(below_diagonal(True), weights, 0.0)
        grads = g_s[at, :]
        slopes = (weights * dot(values, grads, 1, 1)).astype(BF16)
        grad_k = grad_k + dot(slopes, r_s[at, :])
        grad_v = grad_v + dot(weights.astype(BF16), grads)
        dq_s[at, :] += dot(slopes, keys, 0, 0)
        return grad_k, grad_v

    def one(tile, last, after):
        at = pl.ds(pl.multiple_of(tile * TILE, TILE), TILE)
        keys, values = k_s[at, :], v_s[at, :]
        zero = jnp.zeros((TILE, LANES), F32)
        carry = step(keys, values, tile, (zero, zero), True)
        carry = lax.fori_loop(tile + 1, last, lambda j, c: step(keys, values, j, c), carry)
        carry = lax.fori_loop(*after, lambda j, c: step(keys, values, j, c), carry)
        grad_k, grad_v = carry
        for part in range(TILE // block):
            target = order_ref[tile * (TILE // block) + part]
            place = pl.ds(pl.multiple_of(target * block, block), block)
            piece = slice(part * block, (part + 1) * block)
            o_ref[place, LANES:] = jnp.where(low, grad_v[piece], 0.0).astype(BF16)
        dq_s[at, :] += grad_k

    def in_prompt(tile, carry):
        one(tile, prompt // TILE, (prompt // TILE, tokens // TILE))
        return carry

    def in_run(i, carry):
        tile = prompt // TILE + i
        one(tile, prompt // TILE + (lax.div(i, per_run) + 1) * per_run, (0, 0))
        return carry

    lax.fori_loop(0, prompt // TILE, in_prompt, 0)
    lax.fori_loop(0, prompt // TILE, in_run, 0)

    def put(j, carry):
        source = pl.ds(pl.multiple_of(j * block, block), block)
        place = pl.ds(pl.multiple_of(order_ref[j] * block, block), block)
        both = dq_s[source, :] * SCALE
        o_ref[place, :LANES] = turn(both, cos_ref[place, :], -sin_ref[place, :]).astype(BF16)
        return carry

    lax.fori_loop(0, tokens // block, put, 0)


def slopes_of(qkv, scaled, order, cos, sin):
    tokens = qkv.shape[0]
    block = tokens // order.shape[0]
    return pl.pallas_call(
        functools.partial(slopes_kernel, tokens, block),
        out_shape=jax.ShapeDtypeStruct((tokens, 2 * LANES), BF16),
        in_specs=[SMEM_SPEC] + [VMEM_SPEC] * 4,
        out_specs=VMEM_SPEC,
        scratch_shapes=[pltpu.VMEM((tokens, LANES), BF16)] * 5 + [pltpu.VMEM((tokens, LANES), F32)],
        name="slopes",
    )(order, qkv, scaled, cos, sin)


def back_kernel(x_ref, g_ref, u_ref, w_ref, o_ref, gw_ref, gb_ref):
    i = pl.program_id(0)
    merged = g_ref[...]
    o_ref[0] = dot(jnp.concatenate([merged, u_ref[...]], axis=1), w_ref[...], 1, 1).astype(BF16)
    parts = (
        (gw_ref, dot(x_ref[0], merged, 0, 0)),
        (gb_ref, jnp.sum(merged.astype(F32), axis=0, keepdims=True)),
    )

    @pl.when(i == 0)
    def _():
        for ref, value in parts:
            ref[...] = value

    @pl.when(i > 0)
    def _():
        for ref, value in parts:
            ref[...] += value


def back(gathered, merged, grad_up, w_in):
    count, rows, _ = gathered.shape
    whole = lambda shape: pl.BlockSpec(shape, lambda i: (0,) * len(shape))
    by_row = lambda cols: pl.BlockSpec((rows, cols), lambda i: (i, 0))
    by_shard = pl.BlockSpec((1, rows, D), lambda i: (i, 0, 0))
    return pl.pallas_call(
        back_kernel,
        grid=(count,),
        out_shape=[
            jax.ShapeDtypeStruct((count, rows, D), BF16),
            jax.ShapeDtypeStruct((D, 2 * LANES), F32),
            jax.ShapeDtypeStruct((1, 2 * LANES), F32),
        ],
        in_specs=[by_shard, by_row(2 * LANES), by_row(grad_up.shape[1]), whole(w_in.shape)],
        out_specs=[by_shard, whole((D, 2 * LANES)), whole((1, 2 * LANES))],
        name="back",
    )(gathered, merged, grad_up, w_in)


def block_order(table, seg_ids):
    blocks = table.shape[0]
    segment = seg_ids.reshape(blocks, -1)[:, 0]
    number = jnp.arange(blocks, dtype=jnp.int32)
    stored = jnp.sum(jnp.where(table[:, None] == number[None, :], segment[None, :], 0), axis=1)
    key = stored * blocks + table
    rank = jnp.sum((key[None, :] < key[:, None]).astype(jnp.int32), axis=1)
    return jnp.sum(jnp.where(rank[None, :] == number[:, None], number[None, :], 0), axis=1)


def rotary_tables(table, positions):
    blocks = table.shape[0]
    by_block = positions.reshape(blocks, -1)
    number = jnp.arange(blocks, dtype=jnp.int32)
    pick = (table[:, None] == number[None, :])[:, :, None]
    place = jnp.sum(jnp.where(pick, by_block[None], 0), axis=1).reshape(1, -1)
    frequency = 10000.0 ** (-jnp.arange(0, ROT, 2, dtype=F32) / ROT)
    angle = frequency[:, None] * place.astype(F32)
    both = jnp.concatenate([jnp.cos(angle), jnp.sin(angle)], axis=0)
    lane = jnp.arange(LANES) % HDIM
    half = ROT // 2
    row = jnp.arange(half)
    hit = ((lane[None, :] % half) == row[:, None]) & (lane < ROT)[None, :]
    spread_cos = hit.astype(F32)
    spread_sin = jnp.where(lane < half, -1.0, 1.0)[None, :] * spread_cos
    none = jnp.zeros_like(spread_cos)
    spread = jnp.concatenate(
        [jnp.concatenate([spread_cos, none], axis=1), jnp.concatenate([none, spread_sin], axis=1)], axis=0
    )
    tables = lax.dot_general(both, spread, (((0,), (0,)), ((), ())), precision=lax.Precision.HIGHEST)
    return tables[:, :LANES] + (lane >= ROT).astype(F32)[None, :], tables[:, LANES:]


def local(
    tokens, cotangent, w_qkv, w_up, w_out, w_down, b_qkv, b_up, b_out, b_down, ln_gain, ln_bias, block_table, seg_ids, positions,
):
    shards = lax.axis_size("fsdp")
    count = lax.axis_size("ctx")
    me = lax.axis_index("ctx")
    repeat = count // HEADS
    head = me // repeat
    owned = D // shards
    part = FF // count // shards
    units = part * shards
    heads_owned = HEADS // shards

    inputs = tokens[0].astype(F32)
    rows = inputs.shape[0]
    gain = ln_gain.astype(F32)
    centered = inputs - jnp.mean(inputs, axis=-1, keepdims=True)
    rstd = lax.rsqrt(jnp.mean(centered * centered, axis=-1, keepdims=True) + EPS)
    xhat = centered * rstd
    normed = (xhat * gain + ln_bias.astype(F32)).astype(BF16)

    def columns(array, start, size):
        return lax.dynamic_slice_in_dim(array, start, size, axis=array.ndim - 1)

    def unit_columns(array):
        return [columns(array, f * (FF // shards) + part * me, part) for f in range(shards)]

    def head_columns(array):
        return [columns(array, k * D + HDIM * head, HDIM) for k in range(3)]

    pad = jnp.zeros((owned, LANES - HDIM), BF16)
    slice_in = jnp.concatenate(head_columns(w_qkv) + [pad] + unit_columns(w_up), axis=1)
    slice_out = jnp.concatenate(
        [
            lax.dynamic_slice_in_dim(w_down, part * me, part, axis=0),
            lax.dynamic_slice_in_dim(w_out, HDIM * (head % heads_owned), HDIM, axis=0),
        ],
        axis=0,
    )
    order = block_order(block_table[0], seg_ids[0])
    cos, sin = rotary_tables(block_table[0], positions[0])

    gathered, all_in, all_out = first_exchange(normed, slice_in, slice_out, count, shards)
    w_in = all_in.reshape(D, 2 * LANES + units)
    head_rows = lax.dynamic_index_in_dim(all_out[:, part:], head // heads_owned, 0, keepdims=False)
    w_rows = jnp.concatenate(
        [all_out[:, :part].reshape(units, D), head_rows, jnp.zeros((LANES - HDIM, D), BF16)], axis=0
    )
    bias = jnp.concatenate(head_columns(b_qkv.astype(F32)) + [jnp.ones((LANES - HDIM,), F32)])[None]
    unit_bias = jnp.concatenate(unit_columns(b_up.astype(F32)))[None]
    first_of_head = (me % repeat == 0) if repeat > 1 else True
    keep = jnp.where((jnp.arange(LANES) < HDIM) & first_of_head, 1.0, 0.0)[None]

    qkv = project(gathered, w_in[:, : 2 * LANES], bias, cos, sin)
    acc = attend(qkv, order)
    cots = gather(cotangent[0], count, 1)
    partial, grad_up, scaled, g_rows, g_up, g_up_bias, cot_sum = branch(
        acc, gathered, cots, w_in[:, 2 * LANES :], unit_bias, w_rows, keep
    )
    branches = scatter(partial, count, 2)
    output = (inputs + branches + b_out.astype(F32) + b_down.astype(F32)).astype(BF16)

    merged = slopes_of(qkv, scaled, order, cos, sin)
    if repeat > 1:
        merged = jnp.where(first_of_head, merged, jnp.zeros_like(merged))
    back_partial, g_qkv, g_qkv_bias = back(gathered, merged, grad_up, w_in)
    grad_normed = scatter(back_partial, count, 3)

    scaled_grad = grad_normed * gain
    mean_one = jnp.mean(scaled_grad, axis=-1, keepdims=True)
    mean_two = jnp.mean(scaled_grad * xhat, axis=-1, keepdims=True)
    grad_inputs = (scaled_grad - mean_one - xhat * mean_two) * rstd
    input_grad = (cotangent[0].astype(F32) + grad_inputs).astype(BF16)

    send_in = jnp.concatenate([g_qkv[:, :LANES], g_up], axis=1).astype(BF16).reshape(shards, owned, LANES + units)
    v_rows = owned * HDIM // D
    g_v = g_qkv[:, LANES : LANES + HDIM].reshape(shards, D // HDIM, v_rows, HDIM)
    g_v = jnp.swapaxes(g_v, 1, 2).reshape(shards, v_rows, D)
    biases = jnp.concatenate([g_qkv_bias, g_up_bias], axis=1)
    biases = jnp.concatenate([jnp.pad(biases, ((0, 0), (0, D - biases.shape[1]))), cot_sum], axis=0)
    biases_high = biases.astype(BF16)
    biases_low = (biases - biases_high.astype(F32)).astype(BF16)
    bias_rows = jnp.concatenate([biases_high, biases_low, jnp.zeros((12, D), BF16)], axis=0)
    spread = lambda array: jnp.broadcast_to(array[None], (shards,) + array.shape)
    send_out = jnp.concatenate(
        [
            g_rows[:units].reshape(shards, part, D).astype(BF16),
            spread(g_rows[units : units + HDIM].astype(BF16)),
            g_v.astype(BF16),
            spread(bias_rows),
        ],
        axis=1,
    )
    got_in, got_out = grads_exchange(send_in, send_out, count, shards, 4)

    by_head = got_in.reshape(HEADS, repeat, owned, -1)[:, 0]
    qk_grad = by_head[:, :, :LANES].reshape(HEADS, owned, 2, HDIM)
    qk_grad = jnp.transpose(qk_grad, (1, 2, 0, 3)).reshape(owned, 2 * D)
    out_by_head = got_out.reshape(HEADS, repeat, got_out.shape[1], D)[:, 0]
    at_v = part + HDIM
    v_grad = out_by_head[:, at_v : at_v + v_rows].reshape(HEADS, v_rows, D // HDIM, HDIM)
    v_grad = jnp.transpose(v_grad, (2, 1, 0, 3)).reshape(owned, D)
    w_qkv_grad = jnp.concatenate([qk_grad, v_grad], axis=1).astype(F32)
    up_grad = got_in[:, :, LANES:].reshape(count, owned, shards, part)
    w_up_grad = jnp.transpose(up_grad, (1, 2, 0, 3)).reshape(owned, FF).astype(F32)
    w_down_grad = got_out[:, :part].reshape(FF // shards, D).astype(F32)
    mine = lax.axis_index("fsdp")
    out_grad = lax.dynamic_slice_in_dim(out_by_head[:, part : part + HDIM], mine * heads_owned, heads_owned, axis=0)
    w_out_grad = out_grad.reshape(owned, D).astype(F32)

    at_bias = at_v + v_rows
    sums = got_out[:, at_bias : at_bias + 2].astype(F32) + got_out[:, at_bias + 2 : at_bias + 4].astype(F32)
    head_sums = sums[:, 0].reshape(HEADS, repeat, D)[:, 0, : 3 * HDIM].reshape(HEADS, 3, HDIM)
    b_qkv_grad = jnp.swapaxes(head_sums, 0, 1).reshape(3 * D)
    b_up_grad = jnp.transpose(
        sums[:, 0, 2 * LANES : 2 * LANES + units].reshape(count, shards, part), (1, 0, 2)
    ).reshape(FF)
    b_out_grad = sums[0, 1]
    small = lax.psum(
        jnp.stack([jnp.sum(grad_normed * xhat, axis=0), jnp.sum(grad_normed, axis=0)]), ("ctx", "fsdp")
    )
    return (
        output[None], input_grad[None], w_qkv_grad, w_up_grad, w_out_grad, w_down_grad,
        b_qkv_grad, b_up_grad, b_out_grad, b_out_grad, small[0], small[1],
    )


def solution(mesh):
    rows = P("fsdp", None)
    in_specs = (P("fsdp", "ctx", None),) * 2 + (rows,) * 4 + (P(),) * 6 + (rows,) * 3
    out_specs = (P("fsdp", "ctx", None),) * 2 + (rows,) * 4 + (P(),) * 6
    return jax.shard_map(local, mesh=mesh, in_specs=in_specs, out_specs=out_specs, check_vma=False)
```

time: 1210 us -> 638 us (0.53)
  waiting for transfers between devices: 733 us -> 0 us
  Pallas kernels: 0 us -> 474 us
  matrix products: 273 us -> 3.46 us
  blocking collectives: 59.9 us -> 39.5 us
  between operations: 16.3 us -> 1.53 us
    pallas_call x0 -> x10, Pallas kernels: none -> 474 us  [the longest x2 122 us: scatter(): pl.pallas_call(functools.partial(scatter_kernel, count), out_shape=jax.Sh...]
    all_gather x7 -> x0, waiting for transfers between devices: 369 us -> none  [the longest x1 111 us: local(): lax.all_gather(local_out, 'fsdp', axis=0, tiled=True)]
    dot_general x16 -> x1, matrix products: 273 us -> 3.46 us  [rotary_tables(): lax.dot_general(both, spread, (((0,), (0,)), ((), ())), precision=lax.Pre...]
    reduce_scatter x2 -> x0, waiting for transfers between devices: 189 us -> none  [the longest x1 169 us: local(): lax.psum_scatter(jnp.concatenate([contract_first(columns, grad_merged), c...]
    psum x1 -> x0, waiting for transfers between devices: 174 us -> none  [local(): lax.psum(in_share, 'ctx').astype(jnp.float32)]
    another operation x4 -> x2, local copies, waits for them, and re-layouts: 25.5 us -> 0.69 us  [the longest x1 0.61 us: local(): sums[:, 0, 2 * LANES:2 * LANES + units].reshape(count, shards, part)]
    convert_element_type x0 -> x4, local copies, waits for them, and re-layouts: none -> 19.4 us  [the longest x2 19.1 us: local(): jnp.transpose(up_grad, (1, 2, 0, 3)).reshape(owned, FF).astype(F32)]
    all_gather x1 -> x0, blocking collectives: 19.2 us -> none  [local(): all_delta = lax.all_gather(delta_heads, 'ctx', axis=1, tiled=True)]
  transfers between devices with their start and end apart: 10 -> 0, of which waited for: 9 -> 0; matrix products, arithmetic and copies ran while one was open for 30% -> 0% of each run, Pallas kernels for 0% -> 0%
where the time goes in v1:
time: 638 us; the launch traced here: 625 us
  Pallas kernels  474 us (74%)
  local copies, waits for them, and re-layouts  68.9 us (11%)
  blocking collectives  39.5 us (6%)
  other arithmetic  38.4 us (6%)
    pallas_call x2, Pallas kernels, scatter(): pl.pallas_call(functools.partial(scatter_kernel, count), out_shape=jax.Sh...  122 us
    pallas_call x1, Pallas kernels, grads_exchange(): pl.pallas_call(functools.partial(grads_kernel, count, shards), out_shape=...  116 us
    pallas_call x1, Pallas kernels, gather(): pl.pallas_call(functools.partial(gather_kernel, count), out_shape=jax.Sha...  55.7 us
    pallas_call x1, Pallas kernels, first_exchange(): pl.pallas_call(functools.partial(first_kernel, count, shards), out_shape=...  53.3 us
    pallas_call x1, Pallas kernels, slopes_of(): pl.pallas_call(functools.partial(slopes_kernel, tokens, block), out_shape...  39.7 us
    psum x1, blocking collectives, local(): lax.psum(jnp.stack([jnp.sum(grad_normed * xhat, axis=0), jnp.sum(grad_nor...  39.5 us
    pallas_call x1, Pallas kernels, branch(): pl.pallas_call(branch_kernel, grid=(count,), out_shape=[jax.ShapeDtypeStr...  33.2 us
    pallas_call x1, Pallas kernels, attend(): pl.pallas_call(functools.partial(attend_kernel, tokens, block), out_shape...  21 us

profile of v1, /device:TPU:25, one launch (start us, length us, event | category | flops | bytes accessed | tf_op | source)
XLA Modules:
  0.0 625.5 jit_solution(5049578021770103378)
XLA Ops:
  0.7 0.8 convert_element_type.123
  1.4 0.7 convert_element_type.122
  2.1 1.2 convert_reduce_fusion
  3.3 1.3 fusion.16
  4.6 2.1 fusion.9.x_ref
  6.8 1.2 constant_dynamic-slice_fusion.5
  8.0 1.0 constant_dynamic-slice_fusion.3
  9.0 1.1 concatenate.53.a_ref
  10.1 1.0 constant_dynamic-slice_fusion.2
  11.1 0.8 pad_maximum_fusion.2.b_ref
  11.9 53.3 %first_exchange.1 = (bf16[16,256,1024]{2,1,0:T(8,128)(2,1)}, bf16[2,512,512]{2,1,0:T(8,128)(2,1)}, bf16[2,192,1024]{2,1,0:T(8,128)(2,1)}) custom-call(bf16[256,1024]{1,0:T(8,128)(2,1)} %fusion.9.x_ref, bf16[512,512]{1,0:T(8,128)(2,1)} %concatenate.53.a_ref, bf16[192,1024]{1,0:T(8,128)(2,1)} %pad_maximum_fusion.2.b_ref), custom_call_target="tpu_custom_call" | custom-call | tf_op jit(solution)/shard_map/first_exchange/pallas_call | solution.py:224
  65.3 0.2 select_reduce_fusion.2
  65.5 0.2 convert_reduce_fusion.1
  65.7 0.6 select_reduce_fusion.1.order_ref
  66.3 2.2 fusion.39
  68.5 0.8 fusion.42
  69.3 0.6 pad_maximum_fusion.5
  70.1 0.2 select_reduce_fusion
  70.3 0.5 multiply_cosine_fusion
  70.9 3.5 fusion.22
  74.4 2.3 fusion.38
  76.7 14.2 %project.1.x_ref = bf16[4096,256]{1,0:T(8,128)(2,1)} custom-call(bf16[16,256,1024]{2,1,0:T(8,128)(2,1)} %get-tuple-element.27.x_ref, bf16[1024,256]{1,0:T(8,128)(2,1)} %get-tuple-element.90.w_ref, f32[1,256]{1,0:T(1,128)} %bitcast.136, f32[4096,128]{1,0:T(8,128)} %get-tuple-element.83.cos_ref, f32[4096,128]{1,0:T(8,128)} %get-tuple-element.82.sin_ref), custom_call_target="tpu_custom_call" | custom-call | tf_op jit(solution)/shard_map/project/pallas_call | solution.py:502
  90.9 21.0 %attend.1.acc_ref = f32[4096,128]{1,0:T(8,128)} custom-call(s32[32]{0:T(128)} %select_reduce_fusion.1.order_ref, bf16[4096,256]{1,0:T(8,128)(2,1)} %project.1.x_ref), custom_call_target="tpu_custom_call" | custom-call | tf_op jit(solution)/shard_map/attend/pallas_call | solution.py:578
  111.9 55.7 %gather.1.cot_ref = bf16[16,256,1024]{2,1,0:T(8,128)(2,1)} custom-call(bf16[256,1024]{1,0:T(8,128)(2,1)} %bitcast.123), custom_call_target="tpu_custom_call" | custom-call | tf_op jit(solution)/shard_map/gather/pallas_call | solution.py:181
  167.6 0.8 fusion.41
  168.4 0.6 pad_maximum_fusion.6
  169.1 1.1 maximum_maximum_fusion.w_out_ref
  170.3 0.5 compare_select_fusion.4.keep_ref
  170.8 33.2 %branch.1 = (bf16[16,256,1024]{2,1,0:T(8,128)(2,1)}, bf16[4096,256]{1,0:T(8,128)(2,1)}, bf16[4096,128]{1,0:T(8,128)(2,1)}, f32[384,1024]{1,0:T(8,128)}, f32[1024...) custom-call(f32[4096,128]{1,0:T(8,128)} %attend.1.acc_ref, bf16[16,256,1024]{2,1,0:T(8,128)(2,1)} %get-tuple-element.27.x_ref, ...), custom_call_target="tpu_custom_call" | custom-call | tf_op jit(solution)/shard_map/branch/pallas_call | solution.py:646
  204.0 39.7 %slopes.1.g_ref = bf16[4096,256]{1,0:T(8,128)(2,1)} custom-call(s32[32]{0:T(128)} %select_reduce_fusion.1.order_ref, bf16[4096,256]{1,0:T(8,128)(2,1)} %project.1.x_ref, bf16[4096,128]{1,0:T(8,128)(2,1)} %get-tuple-element.31.g_ref, f32[4096,128]{1,0:T(8,128)} %get-tuple-element.83.cos_ref, f32[4096,128]{1,0:T(8,128)} %get-tuple-element.82.sin_ref), custom_call_target="tpu_custom_call" | custom-call | tf_op jit(solution)/shard_map/slopes/pallas_call | solution.py:741
  243.7 18.6 %back.1 = (bf16[16,256,1024]{2,1,0:T(8,128)(2,1)}, f32[1024,256]{1,0:T(8,128)}, f32[1,256]{1,0:T(1,128)}) custom-call(bf16[16,256,1024]{2,1,0:T(8,128)(2,1)} %get-tuple-element.27.x_ref, bf16[4096,256]{1,0:T(8,128)(2,1)} %slopes.1.g_ref, bf16[4096,256]{1,0:T(8,128)(2,1)} %get-tuple-element.32.u_ref, bf16[1024,512]{1,0:T(8,128)(2,1)} %bitcast.119), custom_call_target="tpu_custom_call" | custom-call | tf_op jit(solution)/shard_map/back/pallas_call | solution.py:776
  262.4 53.4 %scatter.3 = f32[256,1024]{1,0:T(8,128)} custom-call(bf16[16,256,1024]{2,1,0:T(8,128)(2,1)} %get-tuple-element.33.p_ref), custom_call_target="tpu_custom_call" | custom-call | tf_op jit(solution)/shard_map/scatter/pallas_call | solution.py:410
  315.8 1.8 fusion.15
  317.6 68.3 %scatter.2 = f32[256,1024]{1,0:T(8,128)} custom-call(bf16[16,256,1024]{2,1,0:T(8,128)(2,1)} %get-tuple-element.30.p_ref), custom_call_target="tpu_custom_call" | custom-call | tf_op jit(solution)/shard_map/scatter/pallas_call | solution.py:410
  386.0 2.8 fusion.21
  389.0 1.0 pad_maximum_fusion.1.a_ref
  390.3 0.2 convert_element_type.138
  390.6 0.1 convert.23
  390.8 1.0 pad_maximum_fusion.b_ref
  391.9 116.2 %grads_exchange.1 = (bf16[16,512,384]{2,1,0:T(8,128)(2,1)}, bf16[16,240,1024]{2,1,0:T(8,128)(2,1)}) custom-call(bf16[2,512,384]{2,1,0:T(8,128)(2,1)} %pad_maximum_fusion.1.a_ref, bf16[2,240,1024]{2,1,0:T(8,128)(2,1)} %pad_maximum_fusion.b_ref), custom_call_target="tpu_custom_call" | custom-call | tf_op jit(solution)/shard_map/grads_exchange/pallas_call | solution.py:465
  508.1 1.3 slice.87
  509.4 1.3 reshape.209
  510.8 2.7 copy.67
  513.4 3.2 reshape.210
  516.7 0.5 copy.56
  517.2 3.1 slice.86
  520.3 2.9 copy.53
  523.2 0.2 copy.54
  523.4 3.6 maximum_convert_fusion
  527.0 6.6 %copy.60 = f32[512,3072]{1,0:T(8,128)} copy(f32[512,3072]{0,1:T(8,128)} %maximum_convert_fusion) | data formatting | bytes 12582912
  533.6 6.5 %slice_convert_fusion = f32[16,512,256]{2,1,0:T(8,128)} fusion(bf16[16,512,384]{2,1,0:T(8,128)(2,1)} %get-tuple-element.40), kind=kLoop, calls=%fused_computation.2 | loop fusion | flops 2097152 | bytes 12582912 | tf_op jit(solution)/shard_map/convert_element_type | solution.py:927
  540.1 10.9 %reshape.216 = f32[16,512,2,128]{3,2,1,0:T(2,128)} reshape(f32[16,512,256]{2,1,0:T(8,128)} %slice_convert_fusion) | data formatting | bytes 16777216 | tf_op jit(solution)/shard_map/convert_element_type | solution.py:927
  551.0 8.2 %copy.57 = f32[512,2,16,128]{3,2,1,0:T(8,128)S(1)} copy(f32[512,2,16,128]{3,1,0,2:T(2,128)} %bitcast.112) | data formatting | bytes 16777216 | tf_op jit(solution)/shard_map/convert_element_type | solution.py:927
  559.2 11.7 %copy.66 = f32[64,8,32,128]{3,1,2,0:T(8,128)} copy(f32[64,8,32,128]{3,2,1,0:T(8,128)S(1)} %bitcast.113) | data formatting | bytes 16777216
  571.0 1.9 slice.89
  572.9 1.6 bitcast_convert_fusion.1
  574.6 2.6 slice.90
  577.2 4.7 bitcast_convert_fusion
  581.9 1.1 convert_add_fusion
  583.2 0.7 reshape.211
  583.9 0.6 copy.59
  584.5 39.5 %psum.7 = f32[2,1024]{1,0:T(2,128)S(1)} all-reduce(f32[2,1024]{1,0:T(2,128)S(1)} %pad_maximum_fusion.4), channel_id=1, replica_groups=mesh['ctx'=16,'fsdp'=2] {'ctx','fsdp'}, use_global_device_ids=true, to_apply=%region_10.11 | all-reduce | flops 2048 | bytes 16384 | tf_op jit(solution)/shard_map/psum | solution.py:941
  624.0 0.6 fusion.40
  624.6 0.6 copy.70
  (84 shorter events, 1.4 us)
Async XLA Ops:
  0.6 9.4 %copy-start = (bf16[512,1024]{1,0:T(8,128)(2,1)S(1)}, bf16[512,1024]{1,0:T(8,128)(2,1)}, u32[]{:S(2)}) copy-start(bf16[512,1024]{1,0:T(8,128)(2,1)} %param.19) | copy-start | bytes 3145732
  9.0 56.2 %copy-start.10 = (s32[1,4096]{1,0:T(1,128)S(1)}, s32[1,4096]{1,0:T(1,128)}, u32[]{:S(2)}) copy-start(s32[1,4096]{1,0:T(1,128)} %param.28) | copy-start | bytes 49156
  9.0 56.3 %copy-start.17 = (s32[1,32]{1,0:T(1,128)S(1)}, s32[1,32]{1,0:T(1,128)}, u32[]{:S(2)}) copy-start(s32[1,32]{1,0:T(1,128)} %param.27) | copy-start | bytes 388
  11.1 59.0 %copy-start.11 = (s32[1,4096]{1,0:T(1,128)S(1)}, s32[1,4096]{1,0:T(1,128)}, u32[]{:S(2)}) copy-start(s32[1,4096]{1,0:T(1,128)} %param.29) | copy-start | bytes 49156
  111.9 57.1 %copy-start.8 = (bf16[2,192,1024]{2,1,0:T(8,128)(2,1)S(1)}, bf16[2,192,1024]{2,1,0:T(8,128)(2,1)}, u32[]{:S(2)}) copy-start(bf16[2,192,1024]{2,1,0:T(8,128)(2,1)} %get-tuple-element.29) | copy-start | bytes 2359300
  262.3 53.4 %copy-start.2 = (bf16[1,256,1024]{2,1,0:T(8,128)(2,1)S(1)}, bf16[1,256,1024]{2,1,0:T(8,128)(2,1)}, u32[]{:S(2)}) copy-start(bf16[1,256,1024]{2,1,0:T(8,128)(2,1)} %param.15) | copy-start | bytes 1572868
  262.3 55.2 %copy-start.13 = (bf16[1024]{0:T(1024)(128)(2,1)S(1)}, bf16[1024]{0:T(1024)(128)(2,1)}, u32[]{:S(2)}) copy-start(bf16[1024]{0:T(1024)(128)(2,1)} %param.24) | copy-start | bytes 6148
  262.4 55.2 %copy-start.14 = (bf16[1024]{0:T(1024)(128)(2,1)S(1)}, bf16[1024]{0:T(1024)(128)(2,1)}, u32[]{:S(2)}) copy-start(bf16[1024]{0:T(1024)(128)(2,1)} %param.23) | copy-start | bytes 6148
  317.6 68.4 %copy-start.3 = (f32[256,1024]{1,0:T(8,128)S(1)}, f32[256,1024]{1,0:T(8,128)}, u32[]{:S(2)}) copy-start(f32[256,1024]{1,0:T(8,128)} %scatter.3) | copy-start | bytes 3145732
  317.6 68.4 %copy-start.4 = (bf16[1,256,1024]{2,1,0:T(8,128)(2,1)S(1)}, bf16[1,256,1024]{2,1,0:T(8,128)(2,1)}, u32[]{:S(2)}) copy-start(bf16[1,256,1024]{2,1,0:T(8,128)(2,1)} %param.16) | copy-start | bytes 1572868
  386.0 2.8 copy-start.6
  386.0 2.9 copy-start.7
  388.8 1.1 copy-start.15
  388.8 1.1 copy-start.16
  388.9 1.1 copy-start.9
  388.9 1.7 copy-start.5
  577.2 48.0 %copy-start.1 = (bf16[512,1024]{1,0:T(8,128)(2,1)S(1)}, bf16[512,1024]{1,0:T(8,128)(2,1)}, u32[]{:S(2)}) copy-start(bf16[512,1024]{1,0:T(8,128)(2,1)} %param.19) | copy-start | bytes 3145732
  584.5 40.7 %copy-start.12 = (f32[1,1,1024]{2,1,0:T(1,128)}, f32[1,1,1024]{2,1,0:T(1,128)S(1)}, u32[]{:S(2)}) copy-start(f32[1,1,1024]{2,1,0:T(1,128)S(1)} %slice.109) | copy-start | bytes 12292
